TPU v7x, 32 devices: a whole 2x2x4 slice. The times are simulated.
32 devices in a mesh: dp: 8 (over z, y), expert: 4 (over x, core).
Axes of the slice: x: 2, y: 2, z: 4, core: 2. Of those that a mesh axis runs over, the one named last changes fastest.
Arguments:
- tokens: bfloat16 [512, 2048], P(('dp', 'expert')), may hold values from -6 to 6
- expert_ids: int32 [512, 8], P(('dp', 'expert')), may hold values from 0 to 15, as said below
- route_weight: float32 [512, 8], P(('dp', 'expert')), may hold values from 0.03 to 0.6
- out_grad: bfloat16 [512, 2048], P(('dp', 'expert')), may hold values from -6 to 6
- gate_weight: bfloat16 [32, 2048, 384], P(('dp', 'expert')), may hold values from -0.125 to 0.125
- up_weight: bfloat16 [32, 2048, 384], P(('dp', 'expert')), may hold values from -0.125 to 0.125
- down_weight: bfloat16 [32, 384, 2048], P(('dp', 'expert')), may hold values from -0.21875 to 0.21875
Outputs:
- layer_out: bfloat16 [512, 2048], P(('dp', 'expert'))
- token_grad: bfloat16 [512, 2048], P(('dp', 'expert'))
- route_grad: float32 [512, 8], P(('dp', 'expert'))
- gate_grad: bfloat16 [32, 2048, 384], P(('dp', 'expert'))
- up_grad: bfloat16 [32, 2048, 384], P(('dp', 'expert'))
- down_grad: bfloat16 [32, 384, 2048], P(('dp', 'expert'))
Inputs may be any that keep to these rules, and one draw needn't show every extreme that they name: `expert_ids`: each row names 8 different experts. The rows of one device name no expert more than 16 times, and one expert is named exactly 16 times by the rows of every device.
All inputs are finite; a program needn't handle non-finite values.
Results may differ from a plain program's by a relative error of at most 0.0071.
Values may be sent and summed in bfloat16 or wider, within the bound.
A program may use at most 128 MiB of HBM per device.

v0:
```python
import jax
import jax.numpy as jnp
from jax import lax
from jax.sharding import PartitionSpec as P


def from_partner(shard, axis, apart):
    return lax.ppermute(shard, axis, [(i, i ^ 1 << apart) for i in range(lax.axis_size(axis))])


def contract(left_op, right_op, left_dim, right_dim):
    return lax.dot_general(
        left_op,
        right_op,
        (((left_dim,), (right_dim,)), ((), ())),
        preferred_element_type=jnp.float32,
    )


def deliver(buffer, dp_size, ex_size, experts, capacity, backward):
    feat_width = buffer.shape[1]
    doubled = jnp.broadcast_to(
        buffer.reshape(experts, 1, capacity, feat_width), (experts, 2, capacity, feat_width)
    )
    doubled = doubled.reshape(dp_size, ex_size, capacity, feat_width)
    if backward:
        arrived = lax.all_to_all(
            lax.all_to_all(doubled, "dp", split_axis=0, concat_axis=0, tiled=True),
            "expert",
            split_axis=1,
            concat_axis=1,
            tiled=True,
        )
    else:
        arrived = lax.all_to_all(
            lax.all_to_all(doubled, "dp", split_axis=0, concat_axis=0, tiled=True),
            "expert",
            split_axis=1,
            concat_axis=1,
            tiled=True,
        )
    return arrived.reshape(-1, feat_width)


def bring_back(partials_in, dp_size, ex_size, experts, capacity, half_index, backward):
    feat_width = partials_in.shape[1]
    if backward:
        partner = from_partner(partials_in, "expert", 0)
    else:
        partner = from_partner(partials_in, "expert", 0)
    summed = (partials_in.astype(jnp.float32) + partner.astype(jnp.float32)).astype(jnp.bfloat16)
    summed = summed.reshape(dp_size, ex_size, capacity, feat_width)
    own_half = lax.dynamic_slice_in_dim(summed, half_index * (capacity // 2), capacity // 2, 2)
    if backward:
        returned = lax.all_to_all(
            lax.all_to_all(own_half, "dp", split_axis=0, concat_axis=0, tiled=True),
            "expert",
            split_axis=1,
            concat_axis=1,
            tiled=True,
        )
    else:
        returned = lax.all_to_all(
            lax.all_to_all(own_half, "dp", split_axis=0, concat_axis=0, tiled=True),
            "expert",
            split_axis=1,
            concat_axis=1,
            tiled=True,
        )
    merged = returned.reshape(experts, capacity, feat_width)
    return merged.reshape(experts * capacity, feat_width)


def body(tokens, expert_ids, route_weight, out_grad, gate_weight, up_weight, down_weight):
    dp_size = lax.axis_size("dp")
    ex_size = lax.axis_size("expert")
    tok_count, feat_width = tokens.shape
    top_count = expert_ids.shape[1]
    experts = dp_size * ex_size // 2
    assigned = tok_count * top_count
    capacity = 2 * (assigned // experts)
    half_index = lax.axis_index("expert") % 2
    flat_ids = expert_ids.reshape(-1)
    onehot = (flat_ids[:, None] == jnp.arange(experts, dtype=jnp.int32)[None, :]).astype(jnp.int32)
    before = jnp.cumsum(onehot, axis=0) - onehot
    slot_ids = jnp.sum(before * onehot, axis=1)
    place_row = flat_ids * capacity + slot_ids
    source = (
        jnp.full((experts * capacity,), -1, jnp.int32)
        .at[place_row]
        .set(jnp.arange(assigned, dtype=jnp.int32))
    )
    filled = source >= 0
    assign = jnp.maximum(source, 0)
    rows_tok = assign // top_count
    send_rows = jnp.where(filled[:, None], tokens[rows_tok], jnp.zeros((), jnp.bfloat16))
    in_rows = deliver(send_rows, dp_size, ex_size, experts, capacity, False)
    w_gate = gate_weight[0]
    w_up = up_weight[0]
    w_down = down_weight[0]
    gate_act = jnp.dot(in_rows, w_gate, preferred_element_type=jnp.float32)
    up_act = jnp.dot(in_rows, w_up, preferred_element_type=jnp.float32)
    sig_gate = jax.nn.sigmoid(gate_act)
    hidden = (gate_act * sig_gate * up_act).astype(jnp.bfloat16)
    partial_value = jnp.dot(hidden, w_down, preferred_element_type=jnp.float32).astype(jnp.bfloat16)
    expert_table = bring_back(partial_value, dp_size, ex_size, experts, capacity, half_index, False)
    expert_rows = expert_table[place_row].reshape(tok_count, top_count, feat_width)
    layer_out = jnp.sum(route_weight[:, :, None] * expert_rows.astype(jnp.float32), axis=1).astype(
        jnp.bfloat16
    )
    route_grad = jnp.einsum("tkd,td->tk", expert_rows, out_grad, preferred_element_type=jnp.float32)
    scaled = (route_weight[:, :, None] * out_grad[:, None, :].astype(jnp.float32)).astype(
        jnp.bfloat16
    )
    scaled = scaled.reshape(assigned, feat_width)
    send_grad = jnp.where(filled[:, None], scaled[assign], jnp.zeros((), jnp.bfloat16))
    grad_rows = deliver(send_grad, dp_size, ex_size, experts, capacity, True)
    hidden_grad = contract(grad_rows, w_down, 1, 1)
    gate_pre = (hidden_grad * up_act * sig_gate * (1.0 + gate_act * (1.0 - sig_gate))).astype(
        jnp.bfloat16
    )
    up_pre = (hidden_grad * gate_act * sig_gate).astype(jnp.bfloat16)
    partial_grad = (contract(gate_pre, w_gate, 1, 1) + contract(up_pre, w_up, 1, 1)).astype(
        jnp.bfloat16
    )
    gate_grad = contract(in_rows, gate_pre, 0, 0).astype(jnp.bfloat16)
    up_grad = contract(in_rows, up_pre, 0, 0).astype(jnp.bfloat16)
    down_grad = contract(hidden, grad_rows, 0, 0).astype(jnp.bfloat16)
    grad_table = bring_back(partial_grad, dp_size, ex_size, experts, capacity, half_index, True)
    expert_grad = grad_table[place_row].reshape(tok_count, top_count, feat_width)
    token_grad = jnp.sum(expert_grad.astype(jnp.float32), axis=1).astype(jnp.bfloat16)
    return (layer_out, token_grad, route_grad, gate_grad[None], up_grad[None], down_grad[None])


def solution(mesh):
    in_specs = (
        P(("dp", "expert"), None),
        P(("dp", "expert"), None),
        P(("dp", "expert"), None),
        P(("dp", "expert"), None),
        P(("dp", "expert"), None, None),
        P(("dp", "expert"), None, None),
        P(("dp", "expert"), None, None),
    )
    out_specs = (
        P(("dp", "expert"), None),
        P(("dp", "expert"), None),
        P(("dp", "expert"), None),
        P(("dp", "expert"), None, None),
        P(("dp", "expert"), None, None),
        P(("dp", "expert"), None, None),
    )
    return jax.shard_map(body, mesh=mesh, in_specs=in_specs, out_specs=out_specs, check_vma=False)
```

profile of v0, /device:TPU:0, one launch (start us, length us, event | category | flops | bytes accessed | tf_op | source)
XLA Modules:
  0.0 294.7 jit_solution(16044852591126099703)
XLA Ops:
  0.6 0.8 broadcast_multiply_fusion
  1.5 0.8 copy.43
  2.3 0.1 mul.76
  2.4 0.1 eq.17
  2.5 0.1 fusion.17
  2.6 0.2 reduce_window_sum.11
  2.7 0.2 select_reduce_fusion
  2.9 1.0 scatter_custom_fusion
  3.9 0.8 copy.41
  4.7 0.1 mul.82
  4.8 0.1 broadcast_in_dim.56
  4.9 0.9 convert_element_type.69
  5.8 0.1 fusion.13
  5.9 1.4 gather_fusion.2
  7.3 2.3 gather_fusion
  9.6 1.4 broadcast_select_fusion
  11.0 0.3 broadcast_in_dim.60
  11.3 55.4 %all_to_all.40 = bf16[8,4,16,2048]{3,2,1,0:T(8,128)(2,1)} all-to-all(bf16[8,4,16,2048]{3,2,1,0:T(8,128)(2,1)S(1)} %bitcast.69), channel_id=1, replica_groups=mesh['dp'=8,'expert'=4] {'dp'}, dimensions={0} | all-to-all | bytes 4194304 | tf_op jit(solution)/shard_map/all_to_all | solution.py:36
  66.8 1.6 broadcast_in_dim.62
  68.4 4.3 %all-to-all-start.4 = ((bf16[8,4,16,2048]{3,2,1,0:T(8,128)(2,1)}), bf16[8,4,16,2048]{3,2,1,0:T(8,128)(2,1)}, u32[]{:S(2)}, u32[]{:S(2)}) async-start(bf16[8,4,16,2048]{3,2,1,0:T(8,128)(2,1)} %bitcast.68), calls=%async_computation.4 | async-start | bytes 4194304 | tf_op jit(solution)/shard_map/all_to_all | solution.py:28
  72.7 3.1 %copy.44 = bf16[8,4,16,2048]{3,2,0,1:T(8,128)(2,1)} copy(bf16[8,4,16,2048]{3,2,1,0:T(8,128)(2,1)} %all_to_all.40) | data formatting | bytes 4194304 | tf_op jit(solution)/shard_map/all_to_all | solution.py:36
  75.9 44.2 %all-to-all-done.4 = bf16[8,4,16,2048]{3,2,1,0:T(8,128)(2,1)} async-done(((bf16[8,4,16,2048]{3,2,1,0:T(8,128)(2,1)}), bf16[8,4,16,2048]{3,2,1,0:T(8,128)(2,1)}, u32[]{:S(2)}, u32[]{:S(2)}) %all-to-all-start.4) | async-done | bytes 2097184 | tf_op jit(solution)/shard_map/all_to_all | solution.py:28
  120.1 4.4 %all-to-all-start.1 = ((bf16[8,4,16,2048]{3,2,0,1:T(8,128)(2,1)}), bf16[8,4,16,2048]{3,2,0,1:T(8,128)(2,1)}, u32[]{:S(2)}, u32[]{:S(2)}) async-start(bf16[8,4,16,2048]{3,2,0,1:T(8,128)(2,1)} %copy.44), calls=%async_computation.1 | async-start | bytes 4194304 | tf_op jit(solution)/shard_map/all_to_all | solution.py:35
  124.5 3.2 %copy.49 = bf16[8,4,16,2048]{3,2,0,1:T(8,128)(2,1)} copy(bf16[8,4,16,2048]{3,2,1,0:T(8,128)(2,1)} %all-to-all-done.4) | data formatting | bytes 4194304 | tf_op jit(solution)/shard_map/all_to_all | solution.py:28
  127.7 22.5 %all-to-all-done.1 = bf16[8,4,16,2048]{3,2,0,1:T(8,128)(2,1)} async-done(((bf16[8,4,16,2048]{3,2,0,1:T(8,128)(2,1)}), bf16[8,4,16,2048]{3,2,0,1:T(8,128)(2,1)}, u32[]{:S(2)}, u32[]{:S(2)}) %all-to-all-start.1) | async-done | bytes 2097184 | tf_op jit(solution)/shard_map/all_to_all | solution.py:35
  150.2 4.4 %all-to-all-start.5 = ((bf16[8,4,16,2048]{3,2,0,1:T(8,128)(2,1)}), bf16[8,4,16,2048]{3,2,0,1:T(8,128)(2,1)}, u32[]{:S(2)}, u32[]{:S(2)}) async-start(bf16[8,4,16,2048]{3,2,0,1:T(8,128)(2,1)} %copy.49), calls=%async_computation.5 | async-start | bytes 4194304 | tf_op jit(solution)/shard_map/all_to_all | solution.py:27
  154.7 1.8 copy.45
  156.6 0.2 copy-done.7
  156.7 2.1 fusion.7
  158.9 2.1 fusion.11
  161.0 19.4 %all-to-all-done.5 = bf16[8,4,16,2048]{3,2,0,1:T(8,128)(2,1)} async-done(((bf16[8,4,16,2048]{3,2,0,1:T(8,128)(2,1)}), bf16[8,4,16,2048]{3,2,0,1:T(8,128)(2,1)}, u32[]{:S(2)}, u32[]{:S(2)}) %all-to-all-start.5) | async-done | bytes 2097184 | tf_op jit(solution)/shard_map/all_to_all | solution.py:27
  180.4 1.8 copy.50
  182.3 0.1 copy-done.15
  182.4 1.5 multiply_convert_fusion
  184.0 2.6 convolution_convert_fusion
  186.6 1.3 fusion.9
  187.9 0.1 copy-done.8
  188.0 2.7 add_convert_fusion.1
  190.7 0.5 collective-permute-start.1
  191.2 3.0 %add_convert_fusion.2 = bf16[512,2048]{1,0:T(8,128)(2,1)S(1)} fusion(bf16[512,2048]{1,0:T(8,128)(2,1)} %collective-permute-done, bf16[512,2048]{1,0:T(8,128)(2,1)} %convolution_convert_fusion), kind=kLoop, calls=%fused_computation.7 | loop fusion | flops 4194304 | bytes 6291456 | tf_op jit(solution)/shard_map/convert_element_type | solution.py:51
  194.2 1.0 constant_dynamic-slice_fusion
  195.2 3.7 %all-to-all-start.2 = ((bf16[8,4,8,2048]{3,2,1,0:T(8,128)(2,1)}), bf16[8,4,8,2048]{3,2,1,0:T(8,128)(2,1)S(1)}, u32[]{:S(2)}, u32[]{:S(2)}) async-start(bf16[8,4,8,2048]{3,2,1,0:T(8,128)(2,1)} %constant_dynamic-slice_fusion), calls=%async_computation.2 | async-start | bytes 2097152 | tf_op jit(solution)/shard_map/all_to_all | solution.py:64
  199.0 3.0 %add_convert_fusion = bf16[512,2048]{1,0:T(8,128)(2,1)S(1)} fusion(bf16[512,2048]{1,0:T(8,128)(2,1)} %collective-permute-done.1, bf16[512,2048]{1,0:T(8,128)(2,1)} %add_convert_fusion.1), kind=kLoop, calls=%fused_computation.5 | loop fusion | flops 4194304 | bytes 6291456 | tf_op jit(solution)/shard_map/convert_element_type | solution.py:51
  202.0 1.0 constant_dynamic-slice_fusion.1
  203.1 21.9 %all-to-all-done.2 = bf16[8,4,8,2048]{3,2,1,0:T(8,128)(2,1)S(1)} async-done(((bf16[8,4,8,2048]{3,2,1,0:T(8,128)(2,1)}), bf16[8,4,8,2048]{3,2,1,0:T(8,128)(2,1)S(1)}, u32[]{:S(2)}, u32[]{:S(2)}) %all-to-all-start.2) | async-done | bytes 1048608 | tf_op jit(solution)/shard_map/all_to_all | solution.py:64
  225.0 4.3 %all-to-all-start.6 = ((bf16[8,4,8,2048]{3,2,1,0:T(8,128)(2,1)}), bf16[8,4,8,2048]{3,2,1,0:T(8,128)(2,1)}, u32[]{:S(2)}, u32[]{:S(2)}) async-start(bf16[8,4,8,2048]{3,2,1,0:T(8,128)(2,1)} %constant_dynamic-slice_fusion.1), calls=%async_computation.6 | async-start | bytes 2097152 | tf_op jit(solution)/shard_map/all_to_all | solution.py:56
  229.3 1.0 copy.46
  230.3 24.5 %all-to-all-done.6 = bf16[8,4,8,2048]{3,2,1,0:T(8,128)(2,1)} async-done(((bf16[8,4,8,2048]{3,2,1,0:T(8,128)(2,1)}), bf16[8,4,8,2048]{3,2,1,0:T(8,128)(2,1)}, u32[]{:S(2)}, u32[]{:S(2)}) %all-to-all-start.6) | async-done | bytes 1048608 | tf_op jit(solution)/shard_map/all_to_all | solution.py:56
  254.8 3.5 %all-to-all-start.3 = ((bf16[8,4,8,2048]{3,2,0,1:T(8,128)(2,1)}), bf16[8,4,8,2048]{3,2,0,1:T(8,128)(2,1)S(1)}, u32[]{:S(2)}, u32[]{:S(2)}) async-start(bf16[8,4,8,2048]{3,2,0,1:T(8,128)(2,1)} %copy.46), calls=%async_computation.3 | async-start | bytes 2097152 | tf_op jit(solution)/shard_map/all_to_all | solution.py:63
  258.4 4.0 %fusion.1 = bf16[1,2048,384]{2,1,0:T(8,128)(2,1)} fusion(bf16[512,2048]{1,0:T(8,128)(2,1)} %bitcast.76, bf16[512,384]{1,0:T(8,128)(2,1)S(1)} %copy-done.10), kind=kOutput, calls=%fused_computation.13 | convolution fusion | flops 806092800 | bytes 4063232 | tf_op jit(solution)/shard_map/dot_general | solution.py:12
  262.4 2.4 copy.51
  264.8 8.0 %all-to-all-done.3 = bf16[8,4,8,2048]{3,2,0,1:T(8,128)(2,1)S(1)} async-done(((bf16[8,4,8,2048]{3,2,0,1:T(8,128)(2,1)}), bf16[8,4,8,2048]{3,2,0,1:T(8,128)(2,1)S(1)}, u32[]{:S(2)}, u32[]{:S(2)}) %all-to-all-start.3) | async-done | bytes 1048608 | tf_op jit(solution)/shard_map/all_to_all | solution.py:63
  272.8 4.3 %all-to-all-start.7 = ((bf16[8,4,8,2048]{3,2,0,1:T(8,128)(2,1)}), bf16[8,4,8,2048]{3,2,0,1:T(8,128)(2,1)}, u32[]{:S(2)}, u32[]{:S(2)}) async-start(bf16[8,4,8,2048]{3,2,0,1:T(8,128)(2,1)} %copy.51), calls=%async_computation.7 | async-start | bytes 2097152 | tf_op jit(solution)/shard_map/all_to_all | solution.py:55
  277.0 3.9 %fusion.2 = bf16[1,384,2048]{2,1,0:T(8,128)(2,1)} fusion(bf16[512,384]{1,0:T(8,128)(2,1)S(1)} %copy-done.12, bf16[512,2048]{1,0:T(8,128)(2,1)} %bitcast.67), kind=kOutput, calls=%fused_computation.14 | convolution fusion | flops 806092800 | bytes 4063232 | tf_op jit(solution)/shard_map/dot_general | solution.py:12
  280.9 2.5 fusion
  283.4 1.3 copy.47
  284.7 0.9 gather_fusion.1
  285.6 0.4 fusion.14
  286.1 0.7 copy.54
  286.7 1.1 multiply_reduce_fusion
  287.8 3.7 %all-to-all-done.7 = bf16[8,4,8,2048]{3,2,0,1:T(8,128)(2,1)} async-done(((bf16[8,4,8,2048]{3,2,0,1:T(8,128)(2,1)}), bf16[8,4,8,2048]{3,2,0,1:T(8,128)(2,1)}, u32[]{:S(2)}, u32[]{:S(2)}) %all-to-all-start.7) | async-done | bytes 1048608 | tf_op jit(solution)/shard_map/all_to_all | solution.py:55
  291.5 1.3 copy.52
  292.8 0.9 gather_fusion.3
  293.7 1.0 bitcast_reduce_fusion
  (39 shorter events, 0.2 us)
Async XLA Ops:
  0.6 181.6 %copy-start = (bf16[1,384,2048]{2,1,0:T(8,128)(2,1)S(1)}, bf16[1,384,2048]{2,1,0:T(8,128)(2,1)}, u32[]{:S(2)}) copy-start(bf16[1,384,2048]{2,1,0:T(8,128)(2,1)} %param.13) | copy-start | bytes 4718596
  5.9 1.4 copy-start.1
  68.4 51.7 %all-to-all-start.4 = ((bf16[8,4,16,2048]{3,2,1,0:T(8,128)(2,1)}), bf16[8,4,16,2048]{3,2,1,0:T(8,128)(2,1)}, u32[]{:S(2)}, u32[]{:S(2)}) async-start(bf16[8,4,16,2048]{3,2,1,0:T(8,128)(2,1)} %bitcast.68), calls=%async_computation.4 | async-start | bytes 4194304 | tf_op jit(solution)/shard_map/all_to_all | solution.py:28
  120.1 30.2 %all-to-all-start.1 = ((bf16[8,4,16,2048]{3,2,0,1:T(8,128)(2,1)}), bf16[8,4,16,2048]{3,2,0,1:T(8,128)(2,1)}, u32[]{:S(2)}, u32[]{:S(2)}) async-start(bf16[8,4,16,2048]{3,2,0,1:T(8,128)(2,1)} %copy.44), calls=%async_computation.1 | async-start | bytes 4194304 | tf_op jit(solution)/shard_map/all_to_all | solution.py:35
  150.2 30.2 %all-to-all-start.5 = ((bf16[8,4,16,2048]{3,2,0,1:T(8,128)(2,1)}), bf16[8,4,16,2048]{3,2,0,1:T(8,128)(2,1)}, u32[]{:S(2)}, u32[]{:S(2)}) async-start(bf16[8,4,16,2048]{3,2,0,1:T(8,128)(2,1)} %copy.49), calls=%async_computation.5 | async-start | bytes 4194304 | tf_op jit(solution)/shard_map/all_to_all | solution.py:27
  154.7 2.0 copy-start.7
  156.5 2.3 copy-start.4
  156.7 2.1 copy-start.6
  180.4 1.9 copy-start.14
  180.4 2.0 copy-start.15
  182.3 1.7 copy-start.2
  183.9 2.6 copy-start.11
  183.9 3.9 %copy-start.9 = (bf16[512,384]{1,0:T(8,128)(2,1)}, bf16[512,384]{1,0:T(8,128)(2,1)S(1)}, u32[]{:S(2)}) copy-start(bf16[512,384]{1,0:T(8,128)(2,1)S(1)} %get-tuple-element.6) | copy-start | bytes 1179652
  186.6 4.6 %collective-permute-start = (bf16[512,2048]{1,0:T(8,128)(2,1)}, bf16[512,2048]{1,0:T(8,128)(2,1)}, u32[]{:S(2)}, u32[]{:S(2)}) collective-permute-start(bf16[512,2048]{1,0:T(8,128)(2,1)} %convolution_convert_fusion), channel_id=1, source_target_pairs={{0,1},{1,0},{2,3},{3,2},{4,5},{5,4},{6,7},{7,6},{8,9},{9,8},{10,11... | collective-permute-start | bytes 6291464 | tf_op jit(solution)/shard_map/ppermute | solution.py:8
  186.6 1.4 copy-start.8
  190.7 8.3 %collective-permute-start.1 = (bf16[512,2048]{1,0:T(8,128)(2,1)}, bf16[512,2048]{1,0:T(8,128)(2,1)}, u32[]{:S(2)}, u32[]{:S(2)}) collective-permute-start(bf16[512,2048]{1,0:T(8,128)(2,1)} %add_convert_fusion.1), channel_id=1, source_target_pairs={{0,1},{1,0},{2,3},{3,2},{4,5},{5,4},{6,7},{7,6},{8,9},{9,8},{10,11... | collective-permute-start | bytes 6291464 | tf_op jit(solution)/shard_map/ppermute | solution.py:8
  195.2 29.7 %all-to-all-start.2 = ((bf16[8,4,8,2048]{3,2,1,0:T(8,128)(2,1)}), bf16[8,4,8,2048]{3,2,1,0:T(8,128)(2,1)S(1)}, u32[]{:S(2)}, u32[]{:S(2)}) async-start(bf16[8,4,8,2048]{3,2,1,0:T(8,128)(2,1)} %constant_dynamic-slice_fusion), calls=%async_computation.2 | async-start | bytes 2097152 | tf_op jit(solution)/shard_map/all_to_all | solution.py:64
  225.0 29.8 %all-to-all-start.6 = ((bf16[8,4,8,2048]{3,2,1,0:T(8,128)(2,1)}), bf16[8,4,8,2048]{3,2,1,0:T(8,128)(2,1)}, u32[]{:S(2)}, u32[]{:S(2)}) async-start(bf16[8,4,8,2048]{3,2,1,0:T(8,128)(2,1)} %constant_dynamic-slice_fusion.1), calls=%async_computation.6 | async-start | bytes 2097152 | tf_op jit(solution)/shard_map/all_to_all | solution.py:56
  229.3 29.1 %copy-start.10 = (bf16[512,384]{1,0:T(8,128)(2,1)S(1)}, bf16[512,384]{1,0:T(8,128)(2,1)}, u32[]{:S(2)}) copy-start(bf16[512,384]{1,0:T(8,128)(2,1)} %copy-done.9) | copy-start | bytes 1179652
  254.8 17.9 %all-to-all-start.3 = ((bf16[8,4,8,2048]{3,2,0,1:T(8,128)(2,1)}), bf16[8,4,8,2048]{3,2,0,1:T(8,128)(2,1)S(1)}, u32[]{:S(2)}, u32[]{:S(2)}) async-start(bf16[8,4,8,2048]{3,2,0,1:T(8,128)(2,1)} %copy.46), calls=%async_computation.3 | async-start | bytes 2097152 | tf_op jit(solution)/shard_map/all_to_all | solution.py:63
  262.4 14.6 %copy-start.12 = (bf16[512,384]{1,0:T(8,128)(2,1)S(1)}, bf16[512,384]{1,0:T(8,128)(2,1)}, u32[]{:S(2)}) copy-start(bf16[512,384]{1,0:T(8,128)(2,1)} %copy-done.11) | copy-start | bytes 1179652
  272.8 8.2 %copy-start.3 = (bf16[8,4,8,2048]{3,2,0,1:T(8,128)(2,1)}, bf16[8,4,8,2048]{3,2,0,1:T(8,128)(2,1)S(1)}, u32[]{:S(2)}) copy-start(bf16[8,4,8,2048]{3,2,0,1:T(8,128)(2,1)S(1)} %all-to-all-done.3) | copy-start | bytes 3145732
  272.8 18.8 %all-to-all-start.7 = ((bf16[8,4,8,2048]{3,2,0,1:T(8,128)(2,1)}), bf16[8,4,8,2048]{3,2,0,1:T(8,128)(2,1)}, u32[]{:S(2)}, u32[]{:S(2)}) async-start(bf16[8,4,8,2048]{3,2,0,1:T(8,128)(2,1)} %copy.51), calls=%async_computation.7 | async-start | bytes 2097152 | tf_op jit(solution)/shard_map/all_to_all | solution.py:55
  277.0 3.9 %copy-start.5 = (bf16[8,4,16,2048]{3,2,1,0:T(8,128)(2,1)S(1)}, bf16[8,4,16,2048]{3,2,1,0:T(8,128)(2,1)}, u32[]{:S(2)}) copy-start(bf16[8,4,16,2048]{3,2,1,0:T(8,128)(2,1)} %copy-done.4) | copy-start | bytes 6291460
  284.7 1.0 copy-start.13
where the time goes:
time: 296 us; the launch traced here: 295 us
  waiting for transfers between devices  144 us (49%)
  blocking collectives  55.4 us (19%)
  local copies, waits for them, and re-layouts  29.6 us (10%)
  starting transfers between devices  29.5 us (10%)
  matrix products  23.2 us (8%)
  other arithmetic  11.8 us (4%)
    all_to_all x1, blocking collectives, deliver(): lax.all_to_all(doubled, 'dp', split_axis=0, concat_axis=0, tiled=True)  55.4 us
    all_to_all x2, waiting for transfers between devices, bring_back(): lax.all_to_all(own_half, 'dp', split_axis=0, concat_axis=0, tiled=True)  46.4 us
    all_to_all x1, waiting for transfers between devices, deliver(): lax.all_to_all(doubled, 'dp', split_axis=0, concat_axis=0, tiled=True)  44.2 us
    all_to_all x2, waiting for transfers between devices, deliver(): lax.all_to_all(lax.all_to_all(doubled, 'dp', split_axis=0, concat_axis=0,...  41.9 us
    dot_general x6, matrix products, contract(): lax.dot_general(left_op, right_op, (((left_dim,), (right_dim,)), ((), ())...  15.8 us
    all_to_all x2, waiting for transfers between devices, bring_back(): lax.all_to_all(lax.all_to_all(own_half, 'dp', split_axis=0, concat_axis=0...  11.7 us
    all_to_all x2, starting transfers between devices, deliver(): lax.all_to_all(lax.all_to_all(doubled, 'dp', split_axis=0, concat_axis=0,...  8.89 us
    all_to_all x2, starting transfers between devices, bring_back(): lax.all_to_all(own_half, 'dp', split_axis=0, concat_axis=0, tiled=True)  8.01 us
  transfers between devices with their start and end apart: 9, of which 7 were waited for; matrix products, arithmetic and copies ran while one was open for 14% of the time, Pallas kernels for 0%

commit v1 on v0

--- a/solution.py
+++ b/solution.py
@@ -24,12 +24,20 @@
     )
     doubled = doubled.reshape(dp_size, ex_size, capacity, feat_width)
     if backward:
-        arrived = lax.all_to_all(
-            lax.all_to_all(doubled, "dp", split_axis=0, concat_axis=0, tiled=True),
-            "expert",
-            split_axis=1,
-            concat_axis=1,
-            tiled=True,
+        arrived = jnp.concatenate(
+            lax.all_to_all(
+                jnp.stack(
+                    jnp.split(
+                        lax.all_to_all(doubled, "dp", split_axis=0, concat_axis=0, tiled=True),
+                        lax.axis_size("expert"),
+                        axis=1,
+                    )
+                ),
+                "expert",
+                0,
+                0,
+            ),
+            axis=1,
         )
     else:
         arrived = lax.all_to_all(

time: 296 us -> 299 us (1.010)
  waiting for transfers between devices: 144 us -> 151 us
  matrix products: 23.2 us -> 19.4 us
    all_to_all x0 -> x1, waiting for transfers between devices: none -> 22.5 us  [deliver(): lax.all_to_all(jnp.stack(jnp.split(lax.all_to_all(doubled, 'dp', split_ax...]
    all_to_all x2 -> x1, waiting for transfers between devices: 41.9 us -> 22.6 us  [deliver(): lax.all_to_all(lax.all_to_all(doubled, 'dp', split_axis=0, concat_axis=0,...]
    all_to_all x2 -> x1, starting transfers between devices: 8.89 us -> 4.45 us  [deliver(): lax.all_to_all(lax.all_to_all(doubled, 'dp', split_axis=0, concat_axis=0,...]
    all_to_all x0 -> x1, starting transfers between devices: none -> 4.44 us  [deliver(): lax.all_to_all(jnp.stack(jnp.split(lax.all_to_all(doubled, 'dp', split_ax...]
    reshape x0 -> x1, local copies, waits for them, and re-layouts: none -> 3.17 us  [deliver(): jnp.concatenate(lax.all_to_all(jnp.stack(jnp.split(lax.all_to_all(doubled...]
    all_to_all x2 -> x1, local copies, waits for them, and re-layouts: 6.33 us -> 3.19 us  [deliver(): lax.all_to_all(doubled, 'dp', split_axis=0, concat_axis=0, tiled=True)]
  transfers between devices with their start and end apart: 9 -> 9, of which waited for: 7 -> 8; matrix products, arithmetic and copies ran while one was open for 14% -> 12% of each run, Pallas kernels for 0% -> 0%
where the time goes in v1:
time: 299 us; the launch traced here: 298 us
  waiting for transfers between devices  151 us (51%)
  blocking collectives  55.4 us (19%)
  local copies, waits for them, and re-layouts  29.1 us (10%)
  starting transfers between devices  28.9 us (10%)
  matrix products  19.4 us (6%)
  other arithmetic  12.7 us (4%)
    all_to_all x1, blocking collectives, deliver(): lax.all_to_all(doubled, 'dp', split_axis=0, concat_axis=0, tiled=True)  55.4 us
    all_to_all x2, waiting for transfers between devices, bring_back(): lax.all_to_all(own_half, 'dp', split_axis=0, concat_axis=0, tiled=True)  47.6 us
    all_to_all x1, waiting for transfers between devices, deliver(): lax.all_to_all(doubled, 'dp', split_axis=0, concat_axis=0, tiled=True)  44 us
    all_to_all x1, waiting for transfers between devices, deliver(): lax.all_to_all(lax.all_to_all(doubled, 'dp', split_axis=0, concat_axis=0,...  22.6 us
    all_to_all x1, waiting for transfers between devices, deliver(): lax.all_to_all(jnp.stack(jnp.split(lax.all_to_all(doubled, 'dp', split_ax...  22.5 us
    dot_general x6, matrix products, contract(): lax.dot_general(left_op, right_op, (((left_dim,), (right_dim,)), ((), ())...  13.9 us
    all_to_all x2, waiting for transfers between devices, bring_back(): lax.all_to_all(lax.all_to_all(own_half, 'dp', split_axis=0, concat_axis=0...  13.3 us
    all_to_all x2, starting transfers between devices, bring_back(): lax.all_to_all(lax.all_to_all(own_half, 'dp', split_axis=0, concat_axis=0...  7.78 us
  transfers between devices with their start and end apart: 9, of which 8 were waited for; matrix products, arithmetic and copies ran while one was open for 12% of the time, Pallas kernels for 0%

profile of v1, /device:TPU:0, one launch (start us, length us, event | category | flops | bytes accessed | tf_op | source)
XLA Modules:
  0.0 297.9 jit_solution(6119601263001688691)
XLA Ops:
  0.6 0.8 broadcast_multiply_fusion
  1.5 0.8 copy.63
  2.3 0.1 mul.76
  2.4 0.1 eq.17
  2.5 0.1 fusion.17
  2.6 0.2 reduce_window_sum.11
  2.7 0.2 select_reduce_fusion
  2.9 1.0 scatter_custom_fusion
  3.9 0.8 copy.61
  4.9 0.9 convert_element_type.69
  5.8 0.1 fusion.13
  5.9 1.4 gather_fusion.2
  7.3 2.3 gather_fusion
  9.6 1.4 broadcast_select_fusion
  11.0 0.3 broadcast_in_dim.62
  11.3 55.4 %all_to_all.40 = bf16[8,4,16,2048]{3,2,1,0:T(8,128)(2,1)} all-to-all(bf16[8,4,16,2048]{3,2,1,0:T(8,128)(2,1)S(1)} %bitcast.84), channel_id=1, replica_groups=mesh['dp'=8,'expert'=4] {'dp'}, dimensions={0} | all-to-all | bytes 4194304 | tf_op jit(solution)/shard_map/all_to_all | solution.py:31
  66.8 1.6 broadcast_in_dim.60
  68.3 4.3 %all-to-all-start = ((bf16[8,4,16,2048]{3,2,1,0:T(8,128)(2,1)}), bf16[8,4,16,2048]{3,2,1,0:T(8,128)(2,1)}, u32[]{:S(2)}, u32[]{:S(2)}) async-start(bf16[8,4,16,2048]{3,2,1,0:T(8,128)(2,1)} %bitcast.83), calls=%async_computation | async-start | bytes 4194304 | tf_op jit(solution)/shard_map/all_to_all | solution.py:44
  72.7 1.7 slice_bitcast_fusion.3
  74.3 1.6 pad_maximum_fusion
  76.0 44.0 %all-to-all-done = bf16[8,4,16,2048]{3,2,1,0:T(8,128)(2,1)} async-done(((bf16[8,4,16,2048]{3,2,1,0:T(8,128)(2,1)}), bf16[8,4,16,2048]{3,2,1,0:T(8,128)(2,1)}, u32[]{:S(2)}, u32[]{:S(2)}) %all-to-all-start) | async-done | bytes 2097184 | tf_op jit(solution)/shard_map/all_to_all | solution.py:44
  120.0 4.4 %all-to-all-start.5 = ((bf16[4,8,1,16,2048]{4,3,1,2,0:T(8,128)(2,1)}), bf16[4,8,1,16,2048]{4,3,1,2,0:T(8,128)(2,1)}, u32[]{:S(2)}, u32[]{:S(2)}) async-start(bf16[4,8,1,16,2048]{4,3,1,2,0:T(8,128)(2,1)} %pad_maximum_fusion), calls=%async_computation.5 | async-start | bytes 4194304 | tf_op jit(solution)/shard_map/all_to_all | solution.py:28
  124.4 3.2 %copy.64 = bf16[8,4,16,2048]{3,2,0,1:T(8,128)(2,1)} copy(bf16[8,4,16,2048]{3,2,1,0:T(8,128)(2,1)} %all-to-all-done) | data formatting | bytes 4194304 | tf_op jit(solution)/shard_map/all_to_all | solution.py:44
  127.6 22.5 %all-to-all-done.5 = bf16[4,8,1,16,2048]{4,3,1,2,0:T(8,128)(2,1)} async-done(((bf16[4,8,1,16,2048]{4,3,1,2,0:T(8,128)(2,1)}), bf16[4,8,1,16,2048]{4,3,1,2,0:T(8,128)(2,1)}, u32[]{:S(2)}, u32[]{:S(2)}) %all-to-all-start.5) | async-done | bytes 2097184 | tf_op jit(solution)/shard_map/all_to_all | solution.py:28
  150.2 4.4 %all-to-all-start.1 = ((bf16[8,4,16,2048]{3,2,0,1:T(8,128)(2,1)}), bf16[8,4,16,2048]{3,2,0,1:T(8,128)(2,1)}, u32[]{:S(2)}, u32[]{:S(2)}) async-start(bf16[8,4,16,2048]{3,2,0,1:T(8,128)(2,1)} %copy.64), calls=%async_computation.1 | async-start | bytes 4194304 | tf_op jit(solution)/shard_map/all_to_all | solution.py:43
  154.6 3.2 %copy.72 = bf16[8,4,1,16,2048]{4,3,1,0,2:T(8,128)(2,1)} copy(bf16[8,4,1,16,2048]{4,3,0,2,1:T(8,128)(2,1)} %bitcast.18) | data formatting | bytes 4194304 | tf_op jit(solution)/shard_map/reshape | solution.py:27
  157.8 22.6 %all-to-all-done.1 = bf16[8,4,16,2048]{3,2,0,1:T(8,128)(2,1)} async-done(((bf16[8,4,16,2048]{3,2,0,1:T(8,128)(2,1)}), bf16[8,4,16,2048]{3,2,0,1:T(8,128)(2,1)}, u32[]{:S(2)}, u32[]{:S(2)}) %all-to-all-start.1) | async-done | bytes 2097184 | tf_op jit(solution)/shard_map/all_to_all | solution.py:43
  180.4 1.7 copy.65
  182.1 1.3 fusion.7
  183.4 0.9 copy-done.8
  184.3 1.3 fusion.11
  185.5 0.3 copy-done.3
  185.9 1.5 multiply_convert_fusion
  187.4 2.6 convolution_convert_fusion
  190.0 1.3 fusion.9
  191.3 0.1 copy-done.10
  191.4 1.3 add_convert_fusion.1
  192.7 0.6 collective-permute-start.1
  193.3 1.2 collective-permute-done
  194.5 3.0 %add_convert_fusion.2 = bf16[512,2048]{1,0:T(8,128)(2,1)S(1)} fusion(bf16[512,2048]{1,0:T(8,128)(2,1)} %collective-permute-done, bf16[512,2048]{1,0:T(8,128)(2,1)} %convolution_convert_fusion), kind=kLoop, calls=%fused_computation.7 | loop fusion | flops 4194304 | bytes 6291456 | tf_op jit(solution)/shard_map/convert_element_type | solution.py:59
  197.5 1.0 constant_dynamic-slice_fusion
  198.6 3.7 %all-to-all-start.2 = ((bf16[8,4,8,2048]{3,2,1,0:T(8,128)(2,1)}), bf16[8,4,8,2048]{3,2,1,0:T(8,128)(2,1)S(1)}, u32[]{:S(2)}, u32[]{:S(2)}) async-start(bf16[8,4,8,2048]{3,2,1,0:T(8,128)(2,1)} %constant_dynamic-slice_fusion), calls=%async_computation.2 | async-start | bytes 2097152 | tf_op jit(solution)/shard_map/all_to_all | solution.py:72
  202.3 2.4 add_convert_fusion
  204.7 1.0 constant_dynamic-slice_fusion.1
  205.7 22.7 %all-to-all-done.2 = bf16[8,4,8,2048]{3,2,1,0:T(8,128)(2,1)S(1)} async-done(((bf16[8,4,8,2048]{3,2,1,0:T(8,128)(2,1)}), bf16[8,4,8,2048]{3,2,1,0:T(8,128)(2,1)S(1)}, u32[]{:S(2)}, u32[]{:S(2)}) %all-to-all-start.2) | async-done | bytes 1048608 | tf_op jit(solution)/shard_map/all_to_all | solution.py:72
  228.4 3.6 %all-to-all-start.6 = ((bf16[8,4,8,2048]{3,2,1,0:T(8,128)(2,1)}), bf16[8,4,8,2048]{3,2,1,0:T(8,128)(2,1)S(1)}, u32[]{:S(2)}, u32[]{:S(2)}) async-start(bf16[8,4,8,2048]{3,2,1,0:T(8,128)(2,1)} %constant_dynamic-slice_fusion.1), calls=%async_computation.6 | async-start | bytes 2097152 | tf_op jit(solution)/shard_map/all_to_all | solution.py:64
  232.0 1.0 copy.66
  233.1 24.9 %all-to-all-done.6 = bf16[8,4,8,2048]{3,2,1,0:T(8,128)(2,1)S(1)} async-done(((bf16[8,4,8,2048]{3,2,1,0:T(8,128)(2,1)}), bf16[8,4,8,2048]{3,2,1,0:T(8,128)(2,1)S(1)}, u32[]{:S(2)}, u32[]{:S(2)}) %all-to-all-start.6) | async-done | bytes 1048608 | tf_op jit(solution)/shard_map/all_to_all | solution.py:64
  258.0 3.5 %all-to-all-start.3 = ((bf16[8,4,8,2048]{3,2,0,1:T(8,128)(2,1)}), bf16[8,4,8,2048]{3,2,0,1:T(8,128)(2,1)S(1)}, u32[]{:S(2)}, u32[]{:S(2)}) async-start(bf16[8,4,8,2048]{3,2,0,1:T(8,128)(2,1)} %copy.66), calls=%async_computation.3 | async-start | bytes 2097152 | tf_op jit(solution)/shard_map/all_to_all | solution.py:71
  261.5 4.0 %fusion.1 = bf16[1,2048,384]{2,1,0:T(8,128)(2,1)} fusion(bf16[512,2048]{1,0:T(8,128)(2,1)} %bitcast.91, bf16[512,384]{1,0:T(8,128)(2,1)S(1)} %copy-done.12), kind=kOutput, calls=%fused_computation.13 | convolution fusion | flops 806092800 | bytes 4063232 | tf_op jit(solution)/shard_map/dot_general | solution.py:12
  265.6 2.5 copy.73
  268.1 7.9 %all-to-all-done.3 = bf16[8,4,8,2048]{3,2,0,1:T(8,128)(2,1)S(1)} async-done(((bf16[8,4,8,2048]{3,2,0,1:T(8,128)(2,1)}), bf16[8,4,8,2048]{3,2,0,1:T(8,128)(2,1)S(1)}, u32[]{:S(2)}, u32[]{:S(2)}) %all-to-all-start.3) | async-done | bytes 1048608 | tf_op jit(solution)/shard_map/all_to_all | solution.py:71
  275.9 4.3 %all-to-all-start.7 = ((bf16[8,4,8,2048]{3,2,0,1:T(8,128)(2,1)}), bf16[8,4,8,2048]{3,2,0,1:T(8,128)(2,1)}, u32[]{:S(2)}, u32[]{:S(2)}) async-start(bf16[8,4,8,2048]{3,2,0,1:T(8,128)(2,1)} %copy.73), calls=%async_computation.7 | async-start | bytes 2097152 | tf_op jit(solution)/shard_map/all_to_all | solution.py:63
  280.2 3.3 %fusion.2 = bf16[1,384,2048]{2,1,0:T(8,128)(2,1)} fusion(bf16[512,384]{1,0:T(8,128)(2,1)} %copy-done.13, bf16[512,2048]{1,0:T(8,128)(2,1)S(1)} %bitcast.82), kind=kOutput, calls=%fused_computation.14 | convolution fusion | flops 806092800 | bytes 4063232 | tf_op jit(solution)/shard_map/dot_general | solution.py:12
  283.5 2.5 fusion
  285.9 0.1 copy.67
  286.1 0.9 gather_fusion.1
  287.0 0.4 fusion.14
  287.4 0.7 copy.76
  288.1 1.1 multiply_reduce_fusion
  289.2 5.5 %all-to-all-done.7 = bf16[8,4,8,2048]{3,2,0,1:T(8,128)(2,1)} async-done(((bf16[8,4,8,2048]{3,2,0,1:T(8,128)(2,1)}), bf16[8,4,8,2048]{3,2,0,1:T(8,128)(2,1)}, u32[]{:S(2)}, u32[]{:S(2)}) %all-to-all-start.7) | async-done | bytes 1048608 | tf_op jit(solution)/shard_map/all_to_all | solution.py:63
  294.7 1.3 copy.74
  296.0 0.9 gather_fusion.3
  296.9 1.0 bitcast_reduce_fusion
  (38 shorter events, 0.4 us)
Async XLA Ops:
  0.6 184.9 %copy-start = (bf16[1,384,2048]{2,1,0:T(8,128)(2,1)S(1)}, bf16[1,384,2048]{2,1,0:T(8,128)(2,1)}, u32[]{:S(2)}) copy-start(bf16[1,384,2048]{2,1,0:T(8,128)(2,1)} %param.13) | copy-start | bytes 4718596
  5.9 1.4 copy-start.2
  68.3 51.7 %all-to-all-start = ((bf16[8,4,16,2048]{3,2,1,0:T(8,128)(2,1)}), bf16[8,4,16,2048]{3,2,1,0:T(8,128)(2,1)}, u32[]{:S(2)}, u32[]{:S(2)}) async-start(bf16[8,4,16,2048]{3,2,1,0:T(8,128)(2,1)} %bitcast.83), calls=%async_computation | async-start | bytes 4194304 | tf_op jit(solution)/shard_map/all_to_all | solution.py:44
  120.0 30.2 %all-to-all-start.5 = ((bf16[4,8,1,16,2048]{4,3,1,2,0:T(8,128)(2,1)}), bf16[4,8,1,16,2048]{4,3,1,2,0:T(8,128)(2,1)}, u32[]{:S(2)}, u32[]{:S(2)}) async-start(bf16[4,8,1,16,2048]{4,3,1,2,0:T(8,128)(2,1)} %pad_maximum_fusion), calls=%async_computation.5 | async-start | bytes 4194304 | tf_op jit(solution)/shard_map/all_to_all | solution.py:28
  150.2 30.2 %all-to-all-start.1 = ((bf16[8,4,16,2048]{3,2,0,1:T(8,128)(2,1)}), bf16[8,4,16,2048]{3,2,0,1:T(8,128)(2,1)}, u32[]{:S(2)}, u32[]{:S(2)}) async-start(bf16[8,4,16,2048]{3,2,0,1:T(8,128)(2,1)} %copy.64), calls=%async_computation.1 | async-start | bytes 4194304 | tf_op jit(solution)/shard_map/all_to_all | solution.py:43
  157.8 24.3 %copy-start.9 = (bf16[1,2048,384]{2,1,0:T(8,128)(2,1)S(1)}, bf16[1,2048,384]{2,1,0:T(8,128)(2,1)}, u32[]{:S(2)}) copy-start(bf16[1,2048,384]{2,1,0:T(8,128)(2,1)} %param.12) | copy-start | bytes 4718596
  182.1 1.3 copy-start.6
  182.1 2.2 copy-start.8
  184.3 1.6 copy-start.3
  187.4 2.6 copy-start.13
  187.4 3.9 %copy-start.11 = (bf16[512,384]{1,0:T(8,128)(2,1)}, bf16[512,384]{1,0:T(8,128)(2,1)S(1)}, u32[]{:S(2)}) copy-start(bf16[512,384]{1,0:T(8,128)(2,1)S(1)} %get-tuple-element.10) | copy-start | bytes 1179652
  190.0 4.5 %collective-permute-start = (bf16[512,2048]{1,0:T(8,128)(2,1)}, bf16[512,2048]{1,0:T(8,128)(2,1)}, u32[]{:S(2)}, u32[]{:S(2)}) collective-permute-start(bf16[512,2048]{1,0:T(8,128)(2,1)} %convolution_convert_fusion), channel_id=1, source_target_pairs={{0,1},{1,0},{2,3},{3,2},{4,5},{5,4},{6,7},{7,6},{8,9},{9,8},{10,11... | collective-permute-start | bytes 6291464 | tf_op jit(solution)/shard_map/ppermute | solution.py:8
  190.0 1.4 copy-start.10
  192.7 9.6 %collective-permute-start.1 = (bf16[512,2048]{1,0:T(8,128)(2,1)S(1)}, bf16[512,2048]{1,0:T(8,128)(2,1)}, u32[]{:S(2)}, u32[]{:S(2)}) collective-permute-start(bf16[512,2048]{1,0:T(8,128)(2,1)S(1)} %add_convert_fusion.1), channel_id=1, source_target_pairs={{0,1},{1,0},{2,3},{3,2},{4,5},{5,4},{6,7},{7,6},{8,9},{9,8},{10,11... | collective-permute-start | bytes 6291464 | tf_op jit(solution)/shard_map/ppermute | solution.py:8
  198.6 29.8 %all-to-all-start.2 = ((bf16[8,4,8,2048]{3,2,1,0:T(8,128)(2,1)}), bf16[8,4,8,2048]{3,2,1,0:T(8,128)(2,1)S(1)}, u32[]{:S(2)}, u32[]{:S(2)}) async-start(bf16[8,4,8,2048]{3,2,1,0:T(8,128)(2,1)} %constant_dynamic-slice_fusion), calls=%async_computation.2 | async-start | bytes 2097152 | tf_op jit(solution)/shard_map/all_to_all | solution.py:72
  228.4 29.6 %all-to-all-start.6 = ((bf16[8,4,8,2048]{3,2,1,0:T(8,128)(2,1)}), bf16[8,4,8,2048]{3,2,1,0:T(8,128)(2,1)S(1)}, u32[]{:S(2)}, u32[]{:S(2)}) async-start(bf16[8,4,8,2048]{3,2,1,0:T(8,128)(2,1)} %constant_dynamic-slice_fusion.1), calls=%async_computation.6 | async-start | bytes 2097152 | tf_op jit(solution)/shard_map/all_to_all | solution.py:64
  232.0 29.5 %copy-start.12 = (bf16[512,384]{1,0:T(8,128)(2,1)S(1)}, bf16[512,384]{1,0:T(8,128)(2,1)}, u32[]{:S(2)}) copy-start(bf16[512,384]{1,0:T(8,128)(2,1)} %copy-done.11) | copy-start | bytes 1179652
  258.0 3.5 %copy-start.5 = (bf16[8,4,8,2048]{3,2,1,0:T(8,128)(2,1)}, bf16[8,4,8,2048]{3,2,1,0:T(8,128)(2,1)S(1)}, u32[]{:S(2)}) copy-start(bf16[8,4,8,2048]{3,2,1,0:T(8,128)(2,1)S(1)} %all-to-all-done.6) | copy-start | bytes 3145732
  258.0 17.9 %all-to-all-start.3 = ((bf16[8,4,8,2048]{3,2,0,1:T(8,128)(2,1)}), bf16[8,4,8,2048]{3,2,0,1:T(8,128)(2,1)S(1)}, u32[]{:S(2)}, u32[]{:S(2)}) async-start(bf16[8,4,8,2048]{3,2,0,1:T(8,128)(2,1)} %copy.66), calls=%async_computation.3 | async-start | bytes 2097152 | tf_op jit(solution)/shard_map/all_to_all | solution.py:71
  265.6 14.6 %copy-start.4 = (bf16[8,4,1,16,2048]{4,3,1,0,2:T(8,128)(2,1)S(1)}, bf16[8,4,1,16,2048]{4,3,1,0,2:T(8,128)(2,1)}, u32[]{:S(2)}) copy-start(bf16[8,4,1,16,2048]{4,3,1,0,2:T(8,128)(2,1)} %copy.72) | copy-start | bytes 6291460
  275.9 18.8 %all-to-all-start.7 = ((bf16[8,4,8,2048]{3,2,0,1:T(8,128)(2,1)}), bf16[8,4,8,2048]{3,2,0,1:T(8,128)(2,1)}, u32[]{:S(2)}, u32[]{:S(2)}) async-start(bf16[8,4,8,2048]{3,2,0,1:T(8,128)(2,1)} %copy.73), calls=%async_computation.7 | async-start | bytes 2097152 | tf_op jit(solution)/shard_map/all_to_all | solution.py:63
  280.2 3.3 %copy-start.7 = (bf16[8,4,16,2048]{3,2,1,0:T(8,128)(2,1)S(1)}, bf16[8,4,16,2048]{3,2,1,0:T(8,128)(2,1)}, u32[]{:S(2)}) copy-start(bf16[8,4,16,2048]{3,2,1,0:T(8,128)(2,1)} %copy-done.6) | copy-start | bytes 6291460
  286.0 1.0 copy-start.14
  296.0 1.9 copy-start.1
